TPU v7x, 256 devices: a whole 4x4x8 slice. The times are simulated.
256 devices in a mesh: blk: 32 (over z, y), view: 8 (over x, core).
Axes of the slice: x: 4, y: 4, z: 8, core: 2. Of those that a mesh axis runs over, the one named last changes fastest.
Arguments:
- estimate: float32 [512, 128, 256], P('blk'), may hold values from 0.3 to 3
- views: float32 [8, 512, 128, 256], P('view', 'blk'), may hold values from 0.3 to 3
- axial_taps: float32 [8, 33], P('view'), may hold values from 0.1 to 1
- lateral_taps: float32 [8, 2, 17], P('view'), may hold values from 0.05 to 1
- cover: int32 [8, 2], P('view'), may hold values from 0 to 512, as said below
Outputs:
- refined: float32 [512, 128, 256], P('blk')
Inputs may be any that keep to these rules, and one draw needn't show every extreme that they name: cover[v, 0] < cover[v, 1]; every first plane is at most 128 and every end at least 384; some view starts at plane 0 and some view ends at 512.
All inputs are finite; a program needn't handle non-finite values.
Results may differ from a plain program's by a relative error of at most 0.00015.
Values sent between devices are 32-bit elements; how exact they have to be, the bound alone decides.
No kernel may reach another device: no remote copies, remote signals or barrier semaphores. Data moves between devices by JAX's collectives and lax.ppermute only.
A program may use at most 64 MiB of HBM per device.

v0:
```python
import jax
import jax.numpy as jnp
from jax import lax
from jax.sharding import PartitionSpec as P

RAD = 8
RZ = 16
ITERS = 2


def padded(block, sides, width):
    for axis, dim in sides:
        count = lax.axis_size(axis)
        forward = [(i, i + 1) for i in range(count - 1)]
        backward = [(target, source) for source, target in forward]
        low = lax.ppermute(
            lax.slice_in_dim(block, block.shape[dim] - width, None, axis=dim), axis, forward
        )
        high = lax.ppermute(lax.slice_in_dim(block, 0, width, axis=dim), axis, backward)
        block = jnp.concatenate([low, block, high], axis=dim)
    return block


def banded(taps, count, reach):
    taps = taps / jnp.sum(taps)
    rows = jnp.arange(count)[:, None]
    cols = jnp.arange(count)[None, :]
    offset = cols - rows
    where_in = jnp.abs(offset) <= reach
    index = jnp.clip(offset + reach, 0, 2 * reach)
    return jnp.where(where_in, jnp.take(taps, index), jnp.float32(0.0))


def local_axial(taps, planes_dev, reach, flipped):
    taps = taps / jnp.sum(taps)
    rows = jnp.arange(planes_dev)[:, None]
    cols = jnp.arange(planes_dev + 2 * reach)[None, :]
    if flipped:
        offset = rows + reach - cols
    else:
        offset = cols - reach - rows
    where_in = jnp.abs(offset) <= reach
    index = jnp.clip(offset + reach, 0, 2 * reach)
    return jnp.where(where_in, jnp.take(taps, index), jnp.float32(0.0))


def local(estimate, views, axial_taps, lateral_taps, cover):
    hi = lax.Precision.HIGHEST
    planes_dev, rows_all, cols_all = estimate.shape
    ky = banded(lateral_taps[0, 0], rows_all, RAD)
    kx = banded(lateral_taps[0, 1], cols_all, RAD)
    planes = lax.axis_index("blk") * planes_dev + jnp.arange(planes_dev)
    inside = (planes >= cover[0, 0]) & (planes < cover[0, 1])
    recorded = views[0]
    kz_ahead = local_axial(axial_taps[0], planes_dev, RZ, False)
    kz_behind = local_axial(axial_taps[0], planes_dev, RZ, True)
    for step in range(ITERS):
        widened = padded(estimate, (("blk", 0),), RZ)
        blurred = jnp.einsum("wc,cyx->wyx", kz_ahead, widened, precision=hi)
        blurred = jnp.einsum("zyx,wx->zyw", blurred, kx, precision=hi)
        blurred = jnp.einsum("zyx,wy->zwx", blurred, ky, precision=hi)
        ratio = recorded / blurred
        back = jnp.einsum("zyx,xw->zyw", ratio, kx, precision=hi)
        back = jnp.einsum("zyx,yw->zwx", back, ky, precision=hi)
        spread = padded(back, (("blk", 0),), RZ)
        returned = jnp.einsum("wc,cyx->wyx", kz_behind, spread, precision=hi)
        log_terms = jnp.where(inside[:, None, None], jnp.log(returned), jnp.float32(0.0))
        total = lax.psum(log_terms, "view")
        estimate = estimate * jnp.exp(total)
    return estimate


def solution(mesh):
    in_specs = (
        P("blk", None, None),
        P("view", "blk", None, None),
        P("view", None),
        P("view", None, None),
        P("view", None),
    )
    out_specs = P("blk", None, None)
    return jax.shard_map(local, mesh=mesh, in_specs=in_specs, out_specs=out_specs, check_vma=False)
```

profile of v0, /device:TPU:8, one launch (start us, length us, event | category | flops | bytes accessed | tf_op | source)
XLA Modules:
  0.0 520.1 jit_solution(3957215918461065242)
XLA Ops:
  6.5 0.0 all-reduce.3.cloned.1.call-start
  6.5 4.1 collective-permute-start.1
  10.6 1.9 collective-permute-start
  12.6 0.1 reshape.362
  12.7 1.3 reduce_sum.27
  13.9 1.3 divide_bitcast_fusion
  15.2 0.0 copy-start.1
  15.2 4.8 gather_fusion.1
  20.0 0.1 reshape.365
  20.1 0.0 copy-done.1
  20.1 0.6 slice_reduce_fusion.1
  20.7 1.2 slice_divide_fusion.1
  21.9 0.7 fusion.312
  22.6 0.7 fusion.313
  23.4 32.7 %collective-permute-done.1 = f32[16,128,256]{2,1,0:T(8,128)} collective-permute-done((f32[16,128,256]{2,1,0:T(8,128)}, f32[16,128,256]{2,1,0:T(8,128)}, u32[]{:S(2)}, u32[]{:S(2)}) %collective-permute-start.1) | collective-permute-done | bytes 2097184 | tf_op jit(solution)/shard_map/ppermute | solution.py:19
  56.1 1.9 collective-permute-done
  58.0 0.0 copy-done
  58.0 3.0 pad_maximum_fusion
  61.1 6.6 %fusion.6 = f32[16,128,256]{2,0,1:T(8,128)S(1)} fusion(f32[48,128,256]{2,1,0:T(8,128)S(1)} %pad_maximum_fusion, f32[16,48]{1,0:T(8,128)S(1)} %reshape.365, s32[48]{0:T(128)S(1)} %iota_add_fusion), kind=kOutput, calls=%fused_computation.11 | convolution fusion | flops 301999872 | bytes 8391872 | tf_op jit(solution)/shard_map/wc,cyx->wyx/dot_general | solution.py:59
  67.6 13.7 %fusion.18 = f32[16,128,256]{2,1,0:T(8,128)S(1)} fusion(f32[16,128,256]{2,0,1:T(8,128)S(1)} %fusion.6, f32[]{:T(128)} %bitcast.55, f32[]{:T(128)} %bitcast.56, f32[]{:T(128)} %bitcast.57, f32[]{:T(128)} %bitcast.58, f32[]{:T(128)} %bitcast.59, f32[]{:T(128)} %bitcast.61, f32[]{:T(128)} %bitcast.60, f32[]{:T(128)} %bitcast.36, f32[]{:T(128)} %bitcast.38, ...), kind=kOutput, calls=%fused_computation.25 | convolution fusion | flops 1613955072 | bytes 4194372 | tf_op jit(solution)/shard_map/zyx,wx->zyw/dot_general | solution.py:60
  81.3 0.0 copy-start.3
  81.4 13.1 %fusion.76 = f32[128,16,256]{2,0,1:T(8,128)S(1)} fusion(f32[16,128,256]{2,1,0:T(8,128)S(1)} %fusion.18, f32[]{:T(128)} %bitcast.24, f32[]{:T(128)} %bitcast.25, f32[]{:T(128)} %bitcast.26, f32[]{:T(128)} %bitcast.27, f32[]{:T(128)} %bitcast.28, f32[]{:T(128)} %bitcast.30, f32[]{:T(128)} %bitcast.29, f32[]{:T(128)} %bitcast.5, f32[]{:T(128)} %bitcast.7, ...), kind=kOutput, calls=%fused_computation.88 | convolution fusion | flops 806141952 | bytes 4194372 | tf_op jit(solution)/shard_map/zyx,wy->zwx/dot_general | solution.py:61
  94.4 0.0 copy-done.3
  94.4 12.7 %fusion.13 = f32[16,128,256]{2,1,0:T(8,128)S(1)} fusion(f32[128,16,256]{2,0,1:T(8,128)S(1)} %fusion.76, f32[1,16,128,256]{3,2,1,0:T(8,128)S(1)} %copy-done.3, f32[]{:T(128)} %bitcast.55, f32[]{:T(128)} %bitcast.56, f32[]{:T(128)} %bitcast.57, f32[]{:T(128)} %bitcast.58, f32[]{:T(128)} %bitcast.59, f32[]{:T(128)} %bitcast.61, f32[]{:T(128)} %bitcast.60, ...), kind=kOutput, calls=%fused_computation.20 | convolution fusion | flops 1614479360 | bytes 6291524 | tf_op jit(solution)/shard_map/zyx,xw->zyw/dot_general | solution.py:63
  107.1 12.7 %convolution_bitcast_fusion.1 = f32[16,128,256]{2,1,0:T(8,128)S(1)} fusion(f32[16,128,256]{2,1,0:T(8,128)S(1)} %fusion.13, f32[]{:T(128)} %bitcast.24, f32[]{:T(128)} %bitcast.25, f32[]{:T(128)} %bitcast.26, f32[]{:T(128)} %bitcast.27, f32[]{:T(128)} %bitcast.28, f32[]{:T(128)} %bitcast.30, f32[]{:T(128)} %bitcast.29, f32[]{:T(128)} %bitcast.5, ...), kind=kOutput, calls=%fused_computation.32 | convolution fusion | flops 806141952 | bytes 4194372 | tf_op jit(solution)/shard_map/zyx,yw->zwx/dot_general | solution.py:64
  119.9 1.9 collective-permute-start.3
  121.8 3.9 collective-permute-start.2
  125.7 0.1 compare_select_fusion.5
  125.8 0.1 reshape.358
  125.9 0.0 copy-start.2
  125.9 4.8 gather_fusion
  130.7 0.1 reshape.361
  130.8 0.0 copy-done.2
  130.8 0.6 fusion.311
  131.3 1.2 compare_and_fusion
  132.5 35.3 %collective-permute-done.3 = f32[16,128,256]{2,1,0:T(8,128)} collective-permute-done((f32[16,128,256]{2,1,0:T(8,128)S(1)}, f32[16,128,256]{2,1,0:T(8,128)}, u32[]{:S(2)}, u32[]{:S(2)}) %collective-permute-start.3) | collective-permute-done | bytes 2097184 | tf_op jit(solution)/shard_map/ppermute | solution.py:19
  167.9 1.2 collective-permute-done.2
  169.0 3.0 pad_maximum_fusion.1
  172.0 7.8 %log_select_fusion.1 = f32[16,128,256]{2,0,1:T(8,128)} fusion(f32[48,128,256]{2,1,0:T(8,128)S(1)} %pad_maximum_fusion.1, pred[16]{0:T(512)(128)(4,1)S(1)} %compare_and_fusion, f32[16,48]{1,0:T(8,128)S(1)} %reshape.361, s32[16]{0:T(128)S(1)} %iota_add_fusion.1), kind=kOutput, calls=%fused_computation.30 | convolution fusion | flops 302524160 | bytes 8391760 | tf_op jit(solution)/shard_map/wc,cyx->wyx/dot_general | solution.py:66
  179.9 0.0 all-reduce.3.cloned.1.call-update
  179.9 0.0 all-reduce.5.cloned.1.call-start
  179.9 80.9 %all-reduce.3.cloned.1.call-done = f32[16,128,256]{2,0,1:T(8,128)} async-done(((f32[16,128,256]{2,0,1:T(8,128)}), f32[16,128,256]{2,0,1:T(8,128)}) %all-reduce.3.cloned.1.call-update) | async-done | bytes 2097168 | tf_op jit(solution)/shard_map/psum | solution.py:68
  260.8 3.6 copy_multiply_fusion
  264.4 2.4 collective-permute-start.5
  266.9 3.8 collective-permute-start.4
  270.7 41.1 %collective-permute-done.5 = f32[16,128,256]{2,0,1:T(8,128)S(1)} collective-permute-done((f32[16,128,256]{2,0,1:T(8,128)S(1)}, f32[16,128,256]{2,0,1:T(8,128)S(1)}, u32[]{:S(2)}, u32[]{:S(2)}) %collective-permute-start.5) | collective-permute-done | bytes 2097184 | tf_op jit(solution)/shard_map/ppermute | solution.py:19
  311.8 2.2 collective-permute-done.4
  313.9 3.1 fusion
  317.1 13.8 %fusion.16 = f32[16,128,256]{2,1,0:T(8,128)S(1)} fusion(f32[16,128,256]{2,0,1:T(8,128)S(1)} %fusion, f32[]{:T(128)} %bitcast.55, f32[]{:T(128)} %bitcast.56, f32[]{:T(128)} %bitcast.57, f32[]{:T(128)} %bitcast.58, f32[]{:T(128)} %bitcast.59, f32[]{:T(128)} %bitcast.61, f32[]{:T(128)} %bitcast.60, f32[]{:T(128)} %bitcast.36, f32[]{:T(128)} %bitcast.38, ...), kind=kOutput, calls=%fused_computation.23 | convolution fusion | flops 1613955072 | bytes 4194372 | tf_op jit(solution)/shard_map/zyx,wx->zyw/dot_general | solution.py:60
  330.8 0.0 copy-start.4
  330.9 12.9 %fusion.73 = f32[128,16,256]{2,0,1:T(8,128)S(1)} fusion(f32[16,128,256]{2,1,0:T(8,128)S(1)} %fusion.16, f32[]{:T(128)} %bitcast.24, f32[]{:T(128)} %bitcast.25, f32[]{:T(128)} %bitcast.26, f32[]{:T(128)} %bitcast.27, f32[]{:T(128)} %bitcast.28, f32[]{:T(128)} %bitcast.30, f32[]{:T(128)} %bitcast.29, f32[]{:T(128)} %bitcast.5, f32[]{:T(128)} %bitcast.7, ...), kind=kOutput, calls=%fused_computation.85 | convolution fusion | flops 806141952 | bytes 4194372 | tf_op jit(solution)/shard_map/zyx,wy->zwx/dot_general | solution.py:61
  343.7 0.0 copy-done.4
  343.7 12.8 %fusion.12 = f32[16,128,256]{2,1,0:T(8,128)S(1)} fusion(f32[128,16,256]{2,0,1:T(8,128)S(1)} %fusion.73, f32[1,16,128,256]{3,2,1,0:T(8,128)S(1)} %copy-done.4, f32[]{:T(128)} %bitcast.55, f32[]{:T(128)} %bitcast.56, f32[]{:T(128)} %bitcast.57, f32[]{:T(128)} %bitcast.58, f32[]{:T(128)} %bitcast.59, f32[]{:T(128)} %bitcast.61, f32[]{:T(128)} %bitcast.60, ...), kind=kOutput, calls=%fused_computation.18 | convolution fusion | flops 1614479360 | bytes 6291524 | tf_op jit(solution)/shard_map/zyx,xw->zyw/dot_general | solution.py:63
  356.5 12.9 %convolution_bitcast_fusion = f32[16,128,256]{2,1,0:T(8,128)S(1)} fusion(f32[16,128,256]{2,1,0:T(8,128)S(1)} %fusion.12, f32[]{:T(128)} %bitcast.24, f32[]{:T(128)} %bitcast.25, f32[]{:T(128)} %bitcast.26, f32[]{:T(128)} %bitcast.27, f32[]{:T(128)} %bitcast.28, f32[]{:T(128)} %bitcast.30, f32[]{:T(128)} %bitcast.29, f32[]{:T(128)} %bitcast.5, f32[]{:T(128)} %bitcast.7, ...), kind=kOutput, calls=%fused_computation.31 | convolution fusion | flops 806141952 | bytes 4194372 | tf_op jit(solution)/shard_map/zyx,yw->zwx/dot_general | solution.py:64
  369.5 1.9 collective-permute-start.7
  371.4 3.9 collective-permute-start.6
  375.3 40.3 %collective-permute-done.7 = f32[16,128,256]{2,1,0:T(8,128)S(1)} collective-permute-done((f32[16,128,256]{2,1,0:T(8,128)S(1)}, f32[16,128,256]{2,1,0:T(8,128)S(1)}, u32[]{:S(2)}, u32[]{:S(2)}) %collective-permute-start.7) | collective-permute-done | bytes 2097184 | tf_op jit(solution)/shard_map/ppermute | solution.py:19
  415.6 1.9 collective-permute-done.6
  417.5 0.7 pad_maximum_fusion.2
  418.2 7.8 %log_select_fusion = f32[16,128,256]{2,0,1:T(8,128)} fusion(f32[48,128,256]{2,1,0:T(8,128)S(1)} %pad_maximum_fusion.2, pred[16]{0:T(512)(128)(4,1)S(1)} %compare_and_fusion, f32[16,48]{1,0:T(8,128)S(1)} %reshape.361, s32[16]{0:T(128)S(1)} %iota_add_fusion.1), kind=kOutput, calls=%fused_computation.29 | convolution fusion | flops 302524160 | bytes 8391760 | tf_op jit(solution)/shard_map/wc,cyx->wyx/dot_general | solution.py:66
  426.0 0.0 all-reduce.5.cloned.1.call-update
  426.1 82.3 %all-reduce.5.cloned.1.call-done = f32[16,128,256]{2,0,1:T(8,128)} async-done(((f32[16,128,256]{2,0,1:T(8,128)}), f32[16,128,256]{2,0,1:T(8,128)}) %all-reduce.5.cloned.1.call-update) | async-done | bytes 2097168 | tf_op jit(solution)/shard_map/psum | solution.py:68
  508.4 2.1 exponential_multiply_fusion
  510.5 2.5 copy.13
  (6 shorter events, 0.0 us)
Async XLA Ops:
  6.5 254.3 %all-reduce.3.cloned.1.call-start = ((), (), s32[]{:S(2)}) async-start(), calls=%async_computation | async-start | bytes 4194304 | tf_op jit(solution)/shard_map/psum | solution.py:68
  6.5 49.6 %collective-permute-start.1 = (f32[16,128,256]{2,1,0:T(8,128)}, f32[16,128,256]{2,1,0:T(8,128)}, u32[]{:S(2)}, u32[]{:S(2)}) collective-permute-start(f32[16,128,256]{2,1,0:T(8,128)} %param.7), channel_id=1, source_target_pairs={{8,0},{16,8},{24,16},{32,24},{40,32},{48,40},{56,48},{64,56},{72,6... | collective-permute-start | bytes 6291464 | tf_op jit(solution)/shard_map/ppermute | solution.py:19
  10.6 47.4 %collective-permute-start = (f32[16,128,256]{2,1,0:T(8,128)}, f32[16,128,256]{2,1,0:T(8,128)}, u32[]{:S(2)}, u32[]{:S(2)}) collective-permute-start(f32[16,128,256]{2,1,0:T(8,128)} %param.7), channel_id=1, source_target_pairs={{0,8},{8,16},{16,24},{24,32},{32,40},{40,48},{48,56},{56,64},{64,7... | collective-permute-start | bytes 6291464 | tf_op jit(solution)/shard_map/ppermute | solution.py:16
  15.2 4.9 copy-start.1
  15.2 42.8 %copy-start = (f32[16,128,256]{2,1,0:T(8,128)S(1)}, f32[16,128,256]{2,1,0:T(8,128)}, u32[]{:S(2)}) copy-start(f32[16,128,256]{2,1,0:T(8,128)} %param.7) | copy-start | bytes 6291460
  81.3 13.1 %copy-start.3 = (f32[1,16,128,256]{3,2,1,0:T(8,128)S(1)}, f32[1,16,128,256]{3,2,1,0:T(8,128)}, u32[]{:S(2)}) copy-start(f32[1,16,128,256]{3,2,1,0:T(8,128)} %param.8) | copy-start | bytes 6291460
  119.9 48.0 %collective-permute-start.3 = (f32[16,128,256]{2,1,0:T(8,128)S(1)}, f32[16,128,256]{2,1,0:T(8,128)}, u32[]{:S(2)}, u32[]{:S(2)}) collective-permute-start(f32[16,128,256]{2,1,0:T(8,128)S(1)} %convolution_bitcast_fusion.1), channel_id=1, source_target_pairs={{8,0},{16,8},{24,16},{32,24},{40,32},{48,40},{56,48},{64,56},{72,6... | collective-permute-start | bytes 6291464 | tf_op jit(solution)/shard_map/ppermute | solution.py:19
  121.8 47.2 %collective-permute-start.2 = (f32[16,128,256]{2,1,0:T(8,128)S(1)}, f32[16,128,256]{2,1,0:T(8,128)}, u32[]{:S(2)}, u32[]{:S(2)}) collective-permute-start(f32[16,128,256]{2,1,0:T(8,128)S(1)} %convolution_bitcast_fusion.1), channel_id=1, source_target_pairs={{0,8},{8,16},{16,24},{24,32},{32,40},{40,48},{48,56},{56,64},{64,7... | collective-permute-start | bytes 6291464 | tf_op jit(solution)/shard_map/ppermute | solution.py:16
  125.9 4.9 copy-start.2
  179.9 328.5 %all-reduce.5.cloned.1.call-start = ((), (), s32[]{:S(2)}) async-start(), calls=%async_computation.1 | async-start | bytes 4194304 | tf_op jit(solution)/shard_map/psum | solution.py:68
  264.4 47.3 %collective-permute-start.5 = (f32[16,128,256]{2,0,1:T(8,128)S(1)}, f32[16,128,256]{2,0,1:T(8,128)S(1)}, u32[]{:S(2)}, u32[]{:S(2)}) collective-permute-start(f32[16,128,256]{2,0,1:T(8,128)S(1)} %copy_multiply_fusion), channel_id=1, source_target_pairs={{8,0},{16,8},{24,16},{32,24},{40,32},{48,40},{56,48},{64,56},{72,6... | collective-permute-start | bytes 6291464 | tf_op jit(solution)/shard_map/ppermute | solution.py:19
  266.9 47.1 %collective-permute-start.4 = (f32[16,128,256]{2,0,1:T(8,128)S(1)}, f32[16,128,256]{2,0,1:T(8,128)S(1)}, u32[]{:S(2)}, u32[]{:S(2)}) collective-permute-start(f32[16,128,256]{2,0,1:T(8,128)S(1)} %copy_multiply_fusion), channel_id=1, source_target_pairs={{0,8},{8,16},{16,24},{24,32},{32,40},{40,48},{48,56},{56,64},{64,7... | collective-permute-start | bytes 6291464 | tf_op jit(solution)/shard_map/ppermute | solution.py:16
  330.8 12.9 %copy-start.4 = (f32[1,16,128,256]{3,2,1,0:T(8,128)S(1)}, f32[1,16,128,256]{3,2,1,0:T(8,128)}, u32[]{:S(2)}) copy-start(f32[1,16,128,256]{3,2,1,0:T(8,128)} %param.8) | copy-start | bytes 6291460
  369.5 46.1 %collective-permute-start.7 = (f32[16,128,256]{2,1,0:T(8,128)S(1)}, f32[16,128,256]{2,1,0:T(8,128)S(1)}, u32[]{:S(2)}, u32[]{:S(2)}) collective-permute-start(f32[16,128,256]{2,1,0:T(8,128)S(1)} %convolution_bitcast_fusion), channel_id=1, source_target_pairs={{8,0},{16,8},{24,16},{32,24},{40,32},{48,40},{56,48},{64,56},{72,6... | collective-permute-start | bytes 6291464 | tf_op jit(solution)/shard_map/ppermute | solution.py:19
  371.4 46.1 %collective-permute-start.6 = (f32[16,128,256]{2,1,0:T(8,128)S(1)}, f32[16,128,256]{2,1,0:T(8,128)S(1)}, u32[]{:S(2)}, u32[]{:S(2)}) collective-permute-start(f32[16,128,256]{2,1,0:T(8,128)S(1)} %convolution_bitcast_fusion), channel_id=1, source_target_pairs={{0,8},{8,16},{16,24},{24,32},{32,40},{40,48},{48,56},{56,64},{64,7... | collective-permute-start | bytes 6291464 | tf_op jit(solution)/shard_map/ppermute | solution.py:16
Sparse Core Ops, SparseCore 0:
  180.0 80.7 all-reduce.2
  426.2 82.1 all-reduce.4
where the time goes:
time: 531 us; the launch traced here: 520 us
  waiting for transfers between devices  320 us (60%)
  matrix products  130 us (24%)
  starting transfers between devices  24 us (5%)
  other arithmetic  18.1 us (3%)
  local copies, waits for them, and re-layouts  14.4 us (3%)
  between operations  13.9 us (3%)
    psum x2, waiting for transfers between devices, local(): total = lax.psum(log_terms, 'view')  163 us
    ppermute x4, waiting for transfers between devices, padded(): lax.ppermute(lax.slice_in_dim(block, 0, width, axis=dim), axis, backward)  149 us
    dot_general x2, matrix products, local(): blurred = jnp.einsum('zyx,wx->zyw', blurred, kx, precision=hi)  27.5 us
    dot_general x2, matrix products, local(): blurred = jnp.einsum('zyx,wy->zwx', blurred, ky, precision=hi)  25.9 us
    dot_general x2, matrix products, local(): back = jnp.einsum('zyx,yw->zwx', back, ky, precision=hi)  25.6 us
    dot_general x2, matrix products, local(): back = jnp.einsum('zyx,xw->zyw', ratio, kx, precision=hi)  25.4 us
    dot_general x2, matrix products, local(): returned = jnp.einsum('wc,cyx->wyx', kz_behind, spread, precision=hi)  15.7 us
    ppermute x4, starting transfers between devices, padded(): lax.ppermute(lax.slice_in_dim(block, block.shape[dim] - width, None, axis...  13.6 us
  transfers between devices with their start and end apart: 10, of which 10 were waited for; matrix products, arithmetic and copies ran while one was open for 3% of the time, Pallas kernels for 0%

commit v1 on v0

--- a/solution.py
+++ b/solution.py
@@ -65,7 +65,9 @@
         spread = padded(back, (("blk", 0),), RZ)
         returned = jnp.einsum("wc,cyx->wyx", kz_behind, spread, precision=hi)
         log_terms = jnp.where(inside[:, None, None], jnp.log(returned), jnp.float32(0.0))
-        total = lax.psum(log_terms, "view")
+        total = log_terms
+        for hop in (1, 2, 4):
+            total = total + lax.ppermute(total, "view", [(dev, dev ^ hop) for dev in range(8)])
         estimate = estimate * jnp.exp(total)
     return estimate
 

time: 531 us -> 569 us (1.072)
  the two profiles are of different devices: /device:TPU:8 before, /device:TPU:132 now
where the time goes in v1:
time: 569 us; the launch traced here: 558 us
  waiting for transfers between devices  371 us (65%)
  matrix products  128 us (22%)
  starting transfers between devices  28 us (5%)
  other arithmetic  16.3 us (3%)
  local copies, waits for them, and re-layouts  14.5 us (3%)
    ppermute x6, waiting for transfers between devices, local(): lax.ppermute(total, 'view', [(dev, dev ^ hop) for dev in range(8)])  197 us
    ppermute x4, waiting for transfers between devices, padded(): lax.ppermute(lax.slice_in_dim(block, 0, width, axis=dim), axis, backward)  151 us
    dot_general x2, matrix products, local(): blurred = jnp.einsum('zyx,wx->zyw', blurred, kx, precision=hi)  27.6 us
    dot_general x2, matrix products, local(): blurred = jnp.einsum('zyx,wy->zwx', blurred, ky, precision=hi)  26.1 us
    dot_general x2, matrix products, local(): back = jnp.einsum('zyx,yw->zwx', back, ky, precision=hi)  25.8 us
    dot_general x2, matrix products, local(): back = jnp.einsum('zyx,xw->zyw', ratio, kx, precision=hi)  25.7 us
    ppermute x4, waiting for transfers between devices, padded(): lax.ppermute(lax.slice_in_dim(block, block.shape[dim] - width, None, axis...  23.2 us
    ppermute x4, starting transfers between devices, padded(): lax.ppermute(lax.slice_in_dim(block, block.shape[dim] - width, None, axis...  13.9 us
  transfers between devices with their start and end apart: 14, of which 14 were waited for; matrix products, arithmetic and copies ran while one was open for 3% of the time, Pallas kernels for 0%

profile of v1, /device:TPU:132, one launch (start us, length us, event | category | flops | bytes accessed | tf_op | source)
XLA Modules:
  0.0 558.2 jit_solution(6982607062518002248)
XLA Ops:
  0.0 4.5 collective-permute-start.1
  4.5 1.9 collective-permute-start
  6.4 0.1 reshape.362
  6.5 1.3 reduce_sum.27
  7.8 1.3 divide_bitcast_fusion
  9.1 4.8 gather_fusion.1
  13.9 0.1 reshape.365
  13.9 0.7 slice_reduce_fusion.1
  14.6 1.3 slice_divide_fusion.1
  16.0 0.7 fusion.312
  16.7 0.7 fusion.313
  17.4 32.2 %collective-permute-done.1 = f32[16,128,256]{2,1,0:T(8,128)} collective-permute-done((f32[16,128,256]{2,1,0:T(8,128)}, f32[16,128,256]{2,1,0:T(8,128)}, u32[]{:S(2)}, u32[]{:S(2)}) %collective-permute-start.1) | collective-permute-done | bytes 2097184 | tf_op jit(solution)/shard_map/ppermute | solution.py:19
  49.6 7.4 %collective-permute-done = f32[16,128,256]{2,1,0:T(8,128)} collective-permute-done((f32[16,128,256]{2,1,0:T(8,128)}, f32[16,128,256]{2,1,0:T(8,128)}, u32[]{:S(2)}, u32[]{:S(2)}) %collective-permute-start) | collective-permute-done | bytes 2097184 | tf_op jit(solution)/shard_map/ppermute | solution.py:16
  57.1 2.8 pad_maximum_fusion
  59.9 6.5 %fusion.6 = f32[16,128,256]{2,0,1:T(8,128)S(1)} fusion(f32[48,128,256]{2,1,0:T(8,128)S(1)} %pad_maximum_fusion, f32[16,48]{1,0:T(8,128)S(1)} %reshape.365, s32[48]{0:T(128)S(1)} %iota_add_fusion), kind=kOutput, calls=%fused_computation.11 | convolution fusion | flops 301999872 | bytes 8391872 | tf_op jit(solution)/shard_map/wc,cyx->wyx/dot_general | solution.py:59
  66.4 13.8 %fusion.18 = f32[16,128,256]{2,1,0:T(8,128)S(1)} fusion(f32[16,128,256]{2,0,1:T(8,128)S(1)} %fusion.6, f32[]{:T(128)} %bitcast.55, f32[]{:T(128)} %bitcast.56, f32[]{:T(128)} %bitcast.57, f32[]{:T(128)} %bitcast.58, f32[]{:T(128)} %bitcast.59, f32[]{:T(128)} %bitcast.61, f32[]{:T(128)} %bitcast.60, f32[]{:T(128)} %bitcast.36, f32[]{:T(128)} %bitcast.38, ...), kind=kOutput, calls=%fused_computation.25 | convolution fusion | flops 1613955072 | bytes 4194372 | tf_op jit(solution)/shard_map/zyx,wx->zyw/dot_general | solution.py:60
  80.3 13.2 %fusion.76 = f32[128,16,256]{2,0,1:T(8,128)S(1)} fusion(f32[16,128,256]{2,1,0:T(8,128)S(1)} %fusion.18, f32[]{:T(128)} %bitcast.24, f32[]{:T(128)} %bitcast.25, f32[]{:T(128)} %bitcast.26, f32[]{:T(128)} %bitcast.27, f32[]{:T(128)} %bitcast.28, f32[]{:T(128)} %bitcast.30, f32[]{:T(128)} %bitcast.29, f32[]{:T(128)} %bitcast.5, f32[]{:T(128)} %bitcast.7, ...), kind=kOutput, calls=%fused_computation.88 | convolution fusion | flops 806141952 | bytes 4194372 | tf_op jit(solution)/shard_map/zyx,wy->zwx/dot_general | solution.py:61
  93.6 12.9 %fusion.13 = f32[16,128,256]{2,1,0:T(8,128)S(1)} fusion(f32[128,16,256]{2,0,1:T(8,128)S(1)} %fusion.76, f32[1,16,128,256]{3,2,1,0:T(8,128)S(1)} %copy-done.4, f32[]{:T(128)} %bitcast.55, f32[]{:T(128)} %bitcast.56, f32[]{:T(128)} %bitcast.57, f32[]{:T(128)} %bitcast.58, f32[]{:T(128)} %bitcast.59, f32[]{:T(128)} %bitcast.61, f32[]{:T(128)} %bitcast.60, ...), kind=kOutput, calls=%fused_computation.20 | convolution fusion | flops 1614479360 | bytes 6291524 | tf_op jit(solution)/shard_map/zyx,xw->zyw/dot_general | solution.py:63
  106.4 12.8 %convolution_bitcast_fusion.1 = f32[16,128,256]{2,1,0:T(8,128)S(1)} fusion(f32[16,128,256]{2,1,0:T(8,128)S(1)} %fusion.13, f32[]{:T(128)} %bitcast.24, f32[]{:T(128)} %bitcast.25, f32[]{:T(128)} %bitcast.26, f32[]{:T(128)} %bitcast.27, f32[]{:T(128)} %bitcast.28, f32[]{:T(128)} %bitcast.30, f32[]{:T(128)} %bitcast.29, f32[]{:T(128)} %bitcast.5, ...), kind=kOutput, calls=%fused_computation.32 | convolution fusion | flops 806141952 | bytes 4194372 | tf_op jit(solution)/shard_map/zyx,yw->zwx/dot_general | solution.py:64
  119.2 1.9 collective-permute-start.3
  121.1 3.9 collective-permute-start.2
  125.1 0.1 compare_select_fusion.5
  125.2 0.1 reshape.358
  125.3 4.8 gather_fusion
  130.1 0.6 fusion.311
  130.7 1.1 compare_and_fusion
  131.9 35.5 %collective-permute-done.3 = f32[16,128,256]{2,1,0:T(8,128)} collective-permute-done((f32[16,128,256]{2,1,0:T(8,128)S(1)}, f32[16,128,256]{2,1,0:T(8,128)}, u32[]{:S(2)}, u32[]{:S(2)}) %collective-permute-start.3) | collective-permute-done | bytes 2097184 | tf_op jit(solution)/shard_map/ppermute | solution.py:19
  167.4 5.2 collective-permute-done.2
  172.6 2.8 pad_maximum_fusion.1
  175.5 6.6 %log_select_fusion.1 = f32[16,128,256]{2,0,1:T(8,128)S(1)} fusion(f32[48,128,256]{2,1,0:T(8,128)S(1)} %pad_maximum_fusion.1, pred[16]{0:T(512)(128)(4,1)S(1)} %compare_and_fusion, f32[16,48]{1,0:T(8,128)S(1)} %reshape.361, s32[16]{0:T(128)S(1)} %iota_add_fusion.1), kind=kOutput, calls=%fused_computation.30 | convolution fusion | flops 302524160 | bytes 8391760 | tf_op jit(solution)/shard_map/wc,cyx->wyx/dot_general | solution.py:66
  182.0 0.1 collective-permute-start.4
  182.1 4.1 collective-permute-done.4
  186.3 0.5 add.143
  186.8 1.3 collective-permute-start.5
  188.1 46.5 %collective-permute-done.5 = f32[16,128,256]{2,0,1:T(8,128)S(1)} collective-permute-done((f32[16,128,256]{2,0,1:T(8,128)S(1)}, f32[16,128,256]{2,0,1:T(8,128)S(1)}, u32[]{:S(2)}, u32[]{:S(2)}) %collective-permute-start.5) | collective-permute-done | bytes 2097184 | tf_op jit(solution)/shard_map/ppermute | solution.py:70
  234.5 0.5 add.144
  235.0 0.6 collective-permute-start.6
  235.6 47.8 %collective-permute-done.6 = f32[16,128,256]{2,0,1:T(8,128)S(1)} collective-permute-done((f32[16,128,256]{2,0,1:T(8,128)S(1)}, f32[16,128,256]{2,0,1:T(8,128)S(1)}, u32[]{:S(2)}, u32[]{:S(2)}) %collective-permute-start.6) | collective-permute-done | bytes 2097184 | tf_op jit(solution)/shard_map/ppermute | solution.py:70
  283.4 1.5 copy_multiply_fusion
  285.0 1.9 collective-permute-start.8
  286.9 4.1 collective-permute-start.7
  291.0 41.8 %collective-permute-done.8 = f32[16,128,256]{2,0,1:T(8,128)S(1)} collective-permute-done((f32[16,128,256]{2,0,1:T(8,128)S(1)}, f32[16,128,256]{2,0,1:T(8,128)S(1)}, u32[]{:S(2)}, u32[]{:S(2)}) %collective-permute-start.8) | collective-permute-done | bytes 2097184 | tf_op jit(solution)/shard_map/ppermute | solution.py:19
  332.8 5.2 collective-permute-done.7
  338.0 3.1 fusion
  341.1 13.8 %fusion.16 = f32[16,128,256]{2,1,0:T(8,128)S(1)} fusion(f32[16,128,256]{2,0,1:T(8,128)S(1)} %fusion, f32[]{:T(128)} %bitcast.55, f32[]{:T(128)} %bitcast.56, f32[]{:T(128)} %bitcast.57, f32[]{:T(128)} %bitcast.58, f32[]{:T(128)} %bitcast.59, f32[]{:T(128)} %bitcast.61, f32[]{:T(128)} %bitcast.60, f32[]{:T(128)} %bitcast.36, f32[]{:T(128)} %bitcast.38, ...), kind=kOutput, calls=%fused_computation.23 | convolution fusion | flops 1613955072 | bytes 4194372 | tf_op jit(solution)/shard_map/zyx,wx->zyw/dot_general | solution.py:60
  354.9 12.9 %fusion.73 = f32[128,16,256]{2,0,1:T(8,128)S(1)} fusion(f32[16,128,256]{2,1,0:T(8,128)S(1)} %fusion.16, f32[]{:T(128)} %bitcast.24, f32[]{:T(128)} %bitcast.25, f32[]{:T(128)} %bitcast.26, f32[]{:T(128)} %bitcast.27, f32[]{:T(128)} %bitcast.28, f32[]{:T(128)} %bitcast.30, f32[]{:T(128)} %bitcast.29, f32[]{:T(128)} %bitcast.5, f32[]{:T(128)} %bitcast.7, ...), kind=kOutput, calls=%fused_computation.85 | convolution fusion | flops 806141952 | bytes 4194372 | tf_op jit(solution)/shard_map/zyx,wy->zwx/dot_general | solution.py:61
  367.8 12.8 %fusion.12 = f32[16,128,256]{2,1,0:T(8,128)S(1)} fusion(f32[128,16,256]{2,0,1:T(8,128)S(1)} %fusion.73, f32[1,16,128,256]{3,2,1,0:T(8,128)S(1)} %copy-done.5, f32[]{:T(128)} %bitcast.55, f32[]{:T(128)} %bitcast.56, f32[]{:T(128)} %bitcast.57, f32[]{:T(128)} %bitcast.58, f32[]{:T(128)} %bitcast.59, f32[]{:T(128)} %bitcast.61, f32[]{:T(128)} %bitcast.60, ...), kind=kOutput, calls=%fused_computation.18 | convolution fusion | flops 1614479360 | bytes 6291524 | tf_op jit(solution)/shard_map/zyx,xw->zyw/dot_general | solution.py:63
  380.7 13.0 %convolution_bitcast_fusion = f32[16,128,256]{2,1,0:T(8,128)S(1)} fusion(f32[16,128,256]{2,1,0:T(8,128)S(1)} %fusion.12, f32[]{:T(128)} %bitcast.24, f32[]{:T(128)} %bitcast.25, f32[]{:T(128)} %bitcast.26, f32[]{:T(128)} %bitcast.27, f32[]{:T(128)} %bitcast.28, f32[]{:T(128)} %bitcast.30, f32[]{:T(128)} %bitcast.29, f32[]{:T(128)} %bitcast.5, f32[]{:T(128)} %bitcast.7, ...), kind=kOutput, calls=%fused_computation.31 | convolution fusion | flops 806141952 | bytes 4194372 | tf_op jit(solution)/shard_map/zyx,yw->zwx/dot_general | solution.py:64
  393.7 1.9 collective-permute-start.10
  395.6 3.9 collective-permute-start.9
  399.5 41.0 %collective-permute-done.10 = f32[16,128,256]{2,1,0:T(8,128)S(1)} collective-permute-done((f32[16,128,256]{2,1,0:T(8,128)S(1)}, f32[16,128,256]{2,1,0:T(8,128)S(1)}, u32[]{:S(2)}, u32[]{:S(2)}) %collective-permute-start.10) | collective-permute-done | bytes 2097184 | tf_op jit(solution)/shard_map/ppermute | solution.py:19
  440.6 5.2 collective-permute-done.9
  445.8 0.7 pad_maximum_fusion.2
  446.5 6.6 %log_select_fusion = f32[16,128,256]{2,0,1:T(8,128)S(1)} fusion(f32[48,128,256]{2,1,0:T(8,128)S(1)} %pad_maximum_fusion.2, pred[16]{0:T(512)(128)(4,1)S(1)} %compare_and_fusion, f32[16,48]{1,0:T(8,128)S(1)} %reshape.361, s32[16]{0:T(128)S(1)} %iota_add_fusion.1), kind=kOutput, calls=%fused_computation.29 | convolution fusion | flops 302524160 | bytes 8391760 | tf_op jit(solution)/shard_map/wc,cyx->wyx/dot_general | solution.py:66
  453.1 0.1 collective-permute-start.11
  453.2 4.1 collective-permute-done.11
  457.3 0.5 add.146
  457.8 1.3 collective-permute-start.12
  459.1 46.5 %collective-permute-done.12 = f32[16,128,256]{2,0,1:T(8,128)S(1)} collective-permute-done((f32[16,128,256]{2,0,1:T(8,128)S(1)}, f32[16,128,256]{2,0,1:T(8,128)S(1)}, u32[]{:S(2)}, u32[]{:S(2)}) %collective-permute-start.12) | collective-permute-done | bytes 2097184 | tf_op jit(solution)/shard_map/ppermute | solution.py:70
  505.6 0.5 add.147
  506.1 0.6 collective-permute-start.13
  506.6 47.8 %collective-permute-done.13 = f32[16,128,256]{2,0,1:T(8,128)S(1)} collective-permute-done((f32[16,128,256]{2,0,1:T(8,128)S(1)}, f32[16,128,256]{2,0,1:T(8,128)S(1)}, u32[]{:S(2)}, u32[]{:S(2)}) %collective-permute-start.13) | collective-permute-done | bytes 2097184 | tf_op jit(solution)/shard_map/ppermute | solution.py:70
  554.5 0.8 exponential_multiply_fusion
  555.3 2.5 copy.13
  (18 shorter events, 0.1 us)
Async XLA Ops:
  0.0 49.6 %collective-permute-start.1 = (f32[16,128,256]{2,1,0:T(8,128)}, f32[16,128,256]{2,1,0:T(8,128)}, u32[]{:S(2)}, u32[]{:S(2)}) collective-permute-start(f32[16,128,256]{2,1,0:T(8,128)} %param.7), channel_id=1, source_target_pairs={{8,0},{16,8},{24,16},{32,24},{40,32},{48,40},{56,48},{64,56},{72,6... | collective-permute-start | bytes 6291464 | tf_op jit(solution)/shard_map/ppermute | solution.py:19
  4.5 52.6 %collective-permute-start = (f32[16,128,256]{2,1,0:T(8,128)}, f32[16,128,256]{2,1,0:T(8,128)}, u32[]{:S(2)}, u32[]{:S(2)}) collective-permute-start(f32[16,128,256]{2,1,0:T(8,128)} %param.7), channel_id=1, source_target_pairs={{0,8},{8,16},{16,24},{24,32},{32,40},{40,48},{48,56},{56,64},{64,7... | collective-permute-start | bytes 6291464 | tf_op jit(solution)/shard_map/ppermute | solution.py:16
  9.1 4.9 copy-start.2
  9.1 48.0 %copy-start = (f32[16,128,256]{2,1,0:T(8,128)S(1)}, f32[16,128,256]{2,1,0:T(8,128)}, u32[]{:S(2)}) copy-start(f32[16,128,256]{2,1,0:T(8,128)} %param.7) | copy-start | bytes 6291460
  80.3 13.3 %copy-start.4 = (f32[1,16,128,256]{3,2,1,0:T(8,128)S(1)}, f32[1,16,128,256]{3,2,1,0:T(8,128)}, u32[]{:S(2)}) copy-start(f32[1,16,128,256]{3,2,1,0:T(8,128)} %param.8) | copy-start | bytes 6291460
  119.2 48.2 %collective-permute-start.3 = (f32[16,128,256]{2,1,0:T(8,128)S(1)}, f32[16,128,256]{2,1,0:T(8,128)}, u32[]{:S(2)}, u32[]{:S(2)}) collective-permute-start(f32[16,128,256]{2,1,0:T(8,128)S(1)} %convolution_bitcast_fusion.1), channel_id=1, source_target_pairs={{8,0},{16,8},{24,16},{32,24},{40,32},{48,40},{56,48},{64,56},{72,6... | collective-permute-start | bytes 6291464 | tf_op jit(solution)/shard_map/ppermute | solution.py:19
  121.1 51.5 %collective-permute-start.2 = (f32[16,128,256]{2,1,0:T(8,128)S(1)}, f32[16,128,256]{2,1,0:T(8,128)}, u32[]{:S(2)}, u32[]{:S(2)}) collective-permute-start(f32[16,128,256]{2,1,0:T(8,128)S(1)} %convolution_bitcast_fusion.1), channel_id=1, source_target_pairs={{0,8},{8,16},{16,24},{24,32},{32,40},{40,48},{48,56},{56,64},{64,7... | collective-permute-start | bytes 6291464 | tf_op jit(solution)/shard_map/ppermute | solution.py:16
  125.3 4.9 copy-start.3
  182.0 4.2 collective-permute-start.4
  186.8 96.7 %copy-start.1 = (f32[16,128,256]{2,1,0:T(8,128)S(1)}, f32[16,128,256]{2,1,0:T(8,128)}, u32[]{:S(2)}) copy-start(f32[16,128,256]{2,1,0:T(8,128)} %param.7) | copy-start | bytes 6291460
  186.8 47.8 %collective-permute-start.5 = (f32[16,128,256]{2,0,1:T(8,128)S(1)}, f32[16,128,256]{2,0,1:T(8,128)S(1)}, u32[]{:S(2)}, u32[]{:S(2)}) collective-permute-start(f32[16,128,256]{2,0,1:T(8,128)S(1)} %add.143), channel_id=1, source_target_pairs={{0,2},{1,3},{2,0},{3,1},{4,6},{5,7},{6,4},{7,5},{8,10},{9,11},{10,... | collective-permute-start | bytes 6291464 | tf_op jit(solution)/shard_map/ppermute | solution.py:70
  235.0 48.4 %collective-permute-start.6 = (f32[16,128,256]{2,0,1:T(8,128)S(1)}, f32[16,128,256]{2,0,1:T(8,128)S(1)}, u32[]{:S(2)}, u32[]{:S(2)}) collective-permute-start(f32[16,128,256]{2,0,1:T(8,128)S(1)} %add.144), channel_id=1, source_target_pairs={{0,4},{1,5},{2,6},{3,7},{4,0},{5,1},{6,2},{7,3},{8,12},{9,13},{10,... | collective-permute-start | bytes 6291464 | tf_op jit(solution)/shard_map/ppermute | solution.py:70
  285.0 47.8 %collective-permute-start.8 = (f32[16,128,256]{2,0,1:T(8,128)S(1)}, f32[16,128,256]{2,0,1:T(8,128)S(1)}, u32[]{:S(2)}, u32[]{:S(2)}) collective-permute-start(f32[16,128,256]{2,0,1:T(8,128)S(1)} %copy_multiply_fusion), channel_id=1, source_target_pairs={{8,0},{16,8},{24,16},{32,24},{40,32},{48,40},{56,48},{64,56},{72,6... | collective-permute-start | bytes 6291464 | tf_op jit(solution)/shard_map/ppermute | solution.py:19
  286.9 51.1 %collective-permute-start.7 = (f32[16,128,256]{2,0,1:T(8,128)S(1)}, f32[16,128,256]{2,0,1:T(8,128)S(1)}, u32[]{:S(2)}, u32[]{:S(2)}) collective-permute-start(f32[16,128,256]{2,0,1:T(8,128)S(1)} %copy_multiply_fusion), channel_id=1, source_target_pairs={{0,8},{8,16},{16,24},{24,32},{32,40},{40,48},{48,56},{56,64},{64,7... | collective-permute-start | bytes 6291464 | tf_op jit(solution)/shard_map/ppermute | solution.py:16
  354.9 12.9 %copy-start.5 = (f32[1,16,128,256]{3,2,1,0:T(8,128)S(1)}, f32[1,16,128,256]{3,2,1,0:T(8,128)}, u32[]{:S(2)}) copy-start(f32[1,16,128,256]{3,2,1,0:T(8,128)} %param.8) | copy-start | bytes 6291460
  393.7 46.9 %collective-permute-start.10 = (f32[16,128,256]{2,1,0:T(8,128)S(1)}, f32[16,128,256]{2,1,0:T(8,128)S(1)}, u32[]{:S(2)}, u32[]{:S(2)}) collective-permute-start(f32[16,128,256]{2,1,0:T(8,128)S(1)} %convolution_bitcast_fusion), channel_id=1, source_target_pairs={{8,0},{16,8},{24,16},{32,24},{40,32},{48,40},{56,48},{64,56},{72,6... | collective-permute-start | bytes 6291464 | tf_op jit(solution)/shard_map/ppermute | solution.py:19
  395.6 50.2 %collective-permute-start.9 = (f32[16,128,256]{2,1,0:T(8,128)S(1)}, f32[16,128,256]{2,1,0:T(8,128)S(1)}, u32[]{:S(2)}, u32[]{:S(2)}) collective-permute-start(f32[16,128,256]{2,1,0:T(8,128)S(1)} %convolution_bitcast_fusion), channel_id=1, source_target_pairs={{0,8},{8,16},{16,24},{24,32},{32,40},{40,48},{48,56},{56,64},{64,7... | collective-permute-start | bytes 6291464 | tf_op jit(solution)/shard_map/ppermute | solution.py:16
  453.1 4.2 collective-permute-start.11
  457.8 47.8 %collective-permute-start.12 = (f32[16,128,256]{2,0,1:T(8,128)S(1)}, f32[16,128,256]{2,0,1:T(8,128)S(1)}, u32[]{:S(2)}, u32[]{:S(2)}) collective-permute-start(f32[16,128,256]{2,0,1:T(8,128)S(1)} %add.146), channel_id=1, source_target_pairs={{0,2},{1,3},{2,0},{3,1},{4,6},{5,7},{6,4},{7,5},{8,10},{9,11},{10,... | collective-permute-start | bytes 6291464 | tf_op jit(solution)/shard_map/ppermute | solution.py:70
  506.1 48.4 %collective-permute-start.13 = (f32[16,128,256]{2,0,1:T(8,128)S(1)}, f32[16,128,256]{2,0,1:T(8,128)S(1)}, u32[]{:S(2)}, u32[]{:S(2)}) collective-permute-start(f32[16,128,256]{2,0,1:T(8,128)S(1)} %add.147), channel_id=1, source_target_pairs={{0,4},{1,5},{2,6},{3,7},{4,0},{5,1},{6,2},{7,3},{8,12},{9,13},{10,... | collective-permute-start | bytes 6291464 | tf_op jit(solution)/shard_map/ppermute | solution.py:70
